TPU v7x, 256 devices: a whole 4x4x8 slice. The times are simulated.
256 devices in a mesh: member: 16 (over x_lo, z), lat: 8 (over y, core), lon: 2 (over x_hi).
Axes of the slice: x: 4 (x_hi: 2, x_lo: 2; x = x_hi * 2 + x_lo), y: 4, z: 8, core: 2. Of those that a mesh axis runs over, the one named last changes fastest.
Arguments:
- state: float32 [32, 5, 2, 256, 1024], P('member', None, None, 'lat', 'lon'), may hold values from -4 to 4
- kick: float32 [32, 5, 2, 256, 1024], P('member', None, None, 'lat', 'lon'), may hold values from -3 to 3
- forcing: float32 [5, 2, 256, 1024], P(None, None, 'lat', 'lon'), may hold values from -4 to 4
- coupling: float32 [2, 5, 5], replicated, may hold values from -3 to 3
- clone_src: int32 [32], replicated, may hold values from 0 to 31, as said below
Outputs:
- advanced: float32 [32, 5, 2, 256, 1024], P('member', None, None, 'lat', 'lon')
Inputs may be any that keep to these rules, and one draw needn't show every extreme that they name: `clone_src`: entry m equals m for a member that is kept; a replaced member names a member that is kept.
All inputs are finite; a program needn't handle non-finite values.
Results may differ from a plain program's by a relative error of at most 0.00012.
Values sent between devices are 32-bit elements; how exact they have to be, the bound alone decides.
A program may use at most 128 MiB of HBM per device.

v0:
```python
import jax
import jax.numpy as jnp
from jax import lax
from jax.sharding import PartitionSpec as P

STEPS = 4


def with_halo(block, sides, width):
    for axis, dim in sides:
        count = lax.axis_size(axis)
        forward = [(i, i + 1) for i in range(count - 1)]
        forward.append((count - 1, 0))
        backward = [(target, source) for source, target in forward]
        low = lax.ppermute(
            lax.slice_in_dim(block, block.shape[dim] - width, None, axis=dim), axis, forward
        )
        high = lax.ppermute(lax.slice_in_dim(block, 0, width, axis=dim), axis, backward)
        block = jnp.concatenate([low, block, high], axis=dim)
    return block


def advance(padded, forcing_c, coupling):
    h = padded.shape[3] - 4
    w = padded.shape[4] - 4

    def part(di, dj):
        return padded[:, :, :, 2 + di : 2 + di + h, 2 + dj : 2 + dj + w]

    centre = part(0, 0)
    along_x = (8.0 * (part(0, 1) - part(0, -1)) - (part(0, 2) - part(0, -2))) / 12.0
    along_y = (8.0 * (part(1, 0) - part(-1, 0)) - (part(2, 0) - part(-2, 0))) / 12.0
    near = part(0, 1) + part(0, -1) + part(1, 0) + part(-1, 0)
    far_sum = part(0, 2) + part(0, -2) + part(2, 0) + part(-2, 0)
    laplace = (16.0 * near - far_sum - 60.0 * centre) / 12.0
    wind_u = centre[:, 0:1]
    wind_v = centre[:, 1:2]
    mixed = jnp.einsum("kvw,mwkij->mvkij", coupling, centre, precision=lax.Precision.HIGHEST)
    return centre + (
        -0.05 * (wind_u * along_x + wind_v * along_y)
        + 0.05 * laplace
        + 0.25 * mixed
        + 0.1 * forcing_c
    )


def shards(state, kick, forcing, coupling, clone_src):
    per_dev = state.shape[0]
    group = lax.axis_index("member")
    sources = lax.dynamic_slice_in_dim(clone_src, group * per_dev, per_dev)
    piece = lax.all_gather(state, "member", axis=0, tiled=True)
    count = piece.shape[0]
    inside = (sources >= 0) & (sources < count)
    rows = jnp.take(piece, jnp.clip(sources, 0, count - 1), axis=0)
    field = jnp.where(inside[:, None, None, None, None], rows, jnp.zeros_like(state))
    field = field + kick
    lat_dev = state.shape[3]
    lat_total = lat_dev * lax.axis_size("lat")
    base = lax.axis_index("lat") * lat_dev

    def zero_rows(values, first_row):
        rows = first_row + jnp.arange(values.shape[3], dtype=jnp.int32)
        keep = (rows >= 0) & (rows < lat_total)
        return jnp.where(keep[:, None], values, 0.0)

    for step in range(STEPS):
        padded = with_halo(field, (("lat", 3), ("lon", 4)), 2)
        padded = zero_rows(padded, base - 2)
        field = advance(padded, forcing, coupling)
    return field


def solution(mesh):
    in_specs = (
        P("member", None, None, "lat", "lon"),
        P("member", None, None, "lat", "lon"),
        P(None, None, "lat", "lon"),
        P(),
        P(),
    )
    out_specs = P("member", None, None, "lat", "lon")
    return jax.shard_map(shards, mesh=mesh, in_specs=in_specs, out_specs=out_specs, check_vma=False)
```

profile of v0, /device:TPU:4, one launch (start us, length us, event | category | flops | bytes accessed | tf_op | source)
XLA Modules:
  0.0 357.4 jit_solution(12120643734006682233)
XLA Ops:
  8.0 231.1 %all-gather.2.cloned.1.call-done = f32[32,5,2,32,512]{4,3,2,1,0:T(8,128)} async-done(((f32[2,5,2,32,512]{4,3,2,1,0:T(8,128)}), f32[32,5,2,32,512]{4,3,2,1,0:T(8,128)}) %all-gather.2.cloned.1.call-update) | async-done | bytes 20971536 | tf_op jit(solution)/shard_map/all_gather | solution.py:51
  239.1 7.6 %gather_fusion = f32[2,5,2,32,512]{4,3,2,1,0:T(8,128)S(1)} fusion(f32[32,5,2,32,512]{4,3,2,1,0:T(8,128)} %all-gather.2.cloned.1.call-done, s32[1024]{0:T(1024)S(1)} %pad_clamp_fusion), kind=kCustom, calls=%fused_computation | custom fusion | bytes 2621448 | tf_op jit(solution)/shard_map/jit(_take)/gather | solution.py:54
  246.7 3.9 %copy_add_fusion = f32[2,5,2,32,512]{4,1,3,0,2:T(8,128)S(1)} fusion(f32[2,5,2,32,512]{4,3,2,1,0:T(8,128)} %param.6, f32[2,5,2,32,512]{4,3,2,1,0:T(8,128)S(1)} %gather_fusion, pred[2]{0:T(512)(128)(4,1)S(1)} %get-tuple-element.5, pred[2]{0:T(512)(128)(4,1)S(1)} %get-tuple-element.31), kind=kLoop, calls=%fused_computation.17 | loop fusion | flops 983040 | bytes 3932164 | tf_op jit(solution)/shard_map/add | solution.py:56
  250.6 2.9 collective-permute-start.1
  253.7 2.6 collective-permute-done
  256.2 1.8 pad_maximum_fusion.11
  260.5 2.7 collective-permute-start.2
  266.5 1.9 maximum_select_fusion
  269.7 6.2 %fusion.7 = f32[2,5,2,32,512]{4,1,3,0,2:T(8,128)S(1)} fusion(f32[2,5,2,36,516]{4,1,3,0,2:T(8,128)S(1)} %maximum_select_fusion, f32[5,2,32,512]{3,0,2,1:T(8,128)S(1)} %copy-done.1, f32[2,2,32,512]{3,2,0,1:T(8,128)S(1)} %get-tuple-element.32, f32[2,2,32,512]{3,2,0,1:T(8,128)S(1)} %get-tuple-element.33, f32[2,5,5,1,1]{2,0,1,4,3:T(2,128)S(1)} %bitcast.50), kind=kOutput, calls=%fused_computation.16 | convolution fusion | flops 28835840 | bytes 23860224 | tf_op jit(solution)/shard_map/kvw,mwkij->mvkij/dot_general | solution.py:38
  276.0 2.9 collective-permute-start.5
  279.0 2.6 collective-permute-done.4
  282.7 2.7 collective-permute-start.6
  288.5 2.7 collective-permute-done.7
  294.6 6.2 %fusion.5 = f32[2,5,2,32,512]{4,1,3,0,2:T(8,128)S(1)} fusion(f32[2,5,2,36,516]{4,1,3,0,2:T(8,128)S(1)} %maximum_select_fusion.1, f32[2,2,32,512]{3,2,0,1:T(8,128)S(1)} %bitcast.58, f32[2,2,32,512]{3,2,0,1:T(8,128)S(1)} %bitcast.55, f32[5,2,32,512]{3,0,2,1:T(8,128)S(1)} %copy-done.2, f32[2,5,5,1,1]{2,0,1,4,3:T(2,128)S(1)} %bitcast.53), kind=kOutput, calls=%fused_computation.13 | convolution fusion | flops 28835840 | bytes 23860224 | tf_op jit(solution)/shard_map/kvw,mwkij->mvkij/dot_general | solution.py:38
  300.9 2.9 collective-permute-start.9
  303.9 2.6 collective-permute-done.8
  308.7 2.8 collective-permute-start.11
  317.5 6.2 %fusion.3 = f32[2,5,2,32,512]{4,1,3,0,2:T(8,128)S(1)} fusion(f32[2,5,2,36,516]{4,1,3,0,2:T(8,128)S(1)} %maximum_select_fusion.2, f32[2,2,32,512]{3,2,0,1:T(8,128)S(1)} %bitcast.59, f32[2,2,32,512]{3,2,0,1:T(8,128)S(1)} %bitcast.56, f32[5,2,32,512]{3,0,2,1:T(8,128)S(1)} %copy-done.3, f32[2,5,5,1,1]{2,0,1,4,3:T(2,128)S(1)} %bitcast.52), kind=kOutput, calls=%fused_computation.10 | convolution fusion | flops 28835840 | bytes 23860224 | tf_op jit(solution)/shard_map/kvw,mwkij->mvkij/dot_general | solution.py:38
  323.8 2.9 collective-permute-start.13
  326.8 2.6 collective-permute-done.12
  330.5 2.7 collective-permute-start.14
  336.4 2.8 collective-permute-done.15
  342.5 6.2 %fusion.1 = f32[2,5,2,32,512]{4,1,3,0,2:T(8,128)S(1)} fusion(f32[2,5,2,36,516]{4,1,3,0,2:T(8,128)S(1)} %maximum_select_fusion.3, f32[2,2,32,512]{3,2,0,1:T(8,128)S(1)} %bitcast.57, f32[2,2,32,512]{3,2,0,1:T(8,128)S(1)} %bitcast.54, f32[5,2,32,512]{3,0,2,1:T(8,128)S(1)} %copy-done.4, f32[2,5,5,1,1]{2,0,1,4,3:T(2,128)S(1)} %bitcast.51), kind=kOutput, calls=%fused_computation.7 | convolution fusion | flops 28835840 | bytes 23860224 | tf_op jit(solution)/shard_map/kvw,mwkij->mvkij/dot_general | solution.py:38
  348.7 1.8 copy.44
  (74 shorter events, 32.0 us)
Async XLA Ops:
  6.5 263.2 %copy-start = (f32[2,5,5]{2,0,1:T(2,128)S(1)}, f32[2,5,5]{2,0,1:T(2,128)}, u32[]{:S(2)}) copy-start(f32[2,5,5]{2,0,1:T(2,128)} %param.8) | copy-start | bytes 604
  6.5 232.6 %all-gather.2.cloned.1.call-start = ((), (), s32[]{:S(2)}) async-start(), calls=%async_computation | async-start | bytes 22282240 | tf_op jit(solution)/shard_map/all_gather | solution.py:51
  246.7 6.9 %copy-start.5 = (f32[5,2,32,512]{3,2,1,0:T(8,128)S(1)}, f32[5,2,32,512]{3,2,1,0:T(8,128)}, u32[]{:S(2)}) copy-start(f32[5,2,32,512]{3,2,1,0:T(8,128)} %param.7) | copy-start | bytes 1966084
  250.6 5.6 %collective-permute-start = (f32[2,5,2,2,512]{4,1,3,0,2:T(8,128)S(1)}, f32[2,5,2,2,512]{4,1,3,0,2:T(8,128)S(1)}, u32[]{:S(2)}, u32[]{:S(2)}) collective-permute-start(f32[2,5,2,2,512]{4,1,3,0,2:T(8,128)S(1)} %get-tuple-element.29), channel_id=1, source_target_pairs={{0,2},{2,4},{4,6},{6,8},{8,10},{10,12},{12,14},{14,0},{1,3},{3,5},... | collective-permute-start | bytes 245768 | tf_op jit(solution)/shard_map/ppermute | solution.py:15
  250.6 5.6 %collective-permute-start.1 = (f32[2,5,2,2,512]{4,1,3,0,2:T(8,128)S(1)}, f32[2,5,2,2,512]{4,1,3,0,2:T(8,128)}, u32[]{:S(2)}, u32[]{:S(2)}) collective-permute-start(f32[2,5,2,2,512]{4,1,3,0,2:T(8,128)S(1)} %get-tuple-element.30), channel_id=1, source_target_pairs={{2,0},{4,2},{6,4},{8,6},{10,8},{12,10},{14,12},{0,14},{3,1},{5,3},... | collective-permute-start | bytes 245768 | tf_op jit(solution)/shard_map/ppermute | solution.py:18
  259.6 6.6 %collective-permute-start.3 = (f32[2,5,2,36,2]{3,4,2,1,0:T(2,128)S(1)}, f32[2,5,2,36,2]{3,4,2,1,0:T(2,128)S(1)}, u32[]{:S(2)}, u32[]{:S(2)}) collective-permute-start(f32[2,5,2,36,2]{3,4,2,1,0:T(2,128)S(1)} %copy.24), channel_id=1, source_target_pairs={{1,0},{0,1},{3,2},{2,3},{5,4},{4,5},{7,6},{6,7},{9,8},{8,9},{11,10... | collective-permute-start | bytes 17288 | tf_op jit(solution)/shard_map/ppermute | solution.py:18
  260.5 5.3 %collective-permute-start.2 = (f32[2,5,2,36,2]{3,4,2,1,0:T(2,128)S(1)}, f32[2,5,2,36,2]{3,4,2,1,0:T(2,128)S(1)}, u32[]{:S(2)}, u32[]{:S(2)}) collective-permute-start(f32[2,5,2,36,2]{3,4,2,1,0:T(2,128)S(1)} %copy.23), channel_id=1, source_target_pairs={{0,1},{1,0},{2,3},{3,2},{4,5},{5,4},{6,7},{7,6},{8,9},{9,8},{10,11... | collective-permute-start | bytes 17288 | tf_op jit(solution)/shard_map/ppermute | solution.py:15
  268.5 1.2 copy-start.1
  276.0 5.6 %collective-permute-start.4 = (f32[2,5,2,2,512]{4,1,3,0,2:T(8,128)S(1)}, f32[2,5,2,2,512]{4,1,3,0,2:T(8,128)S(1)}, u32[]{:S(2)}, u32[]{:S(2)}) collective-permute-start(f32[2,5,2,2,512]{4,1,3,0,2:T(8,128)S(1)} %get-tuple-element.27), channel_id=1, source_target_pairs={{0,2},{2,4},{4,6},{6,8},{8,10},{10,12},{12,14},{14,0},{1,3},{3,5},... | collective-permute-start | bytes 245768 | tf_op jit(solution)/shard_map/ppermute | solution.py:15
  276.0 5.6 %collective-permute-start.5 = (f32[2,5,2,2,512]{4,1,3,0,2:T(8,128)S(1)}, f32[2,5,2,2,512]{4,1,3,0,2:T(8,128)S(1)}, u32[]{:S(2)}, u32[]{:S(2)}) collective-permute-start(f32[2,5,2,2,512]{4,1,3,0,2:T(8,128)S(1)} %get-tuple-element.28), channel_id=1, source_target_pairs={{2,0},{4,2},{6,4},{8,6},{10,8},{12,10},{14,12},{0,14},{3,1},{5,3},... | collective-permute-start | bytes 245768 | tf_op jit(solution)/shard_map/ppermute | solution.py:18
  282.7 5.5 %collective-permute-start.6 = (f32[2,5,2,36,2]{3,4,2,1,0:T(2,128)}, f32[2,5,2,36,2]{3,4,2,1,0:T(2,128)S(1)}, u32[]{:S(2)}, u32[]{:S(2)}) collective-permute-start(f32[2,5,2,36,2]{3,4,2,1,0:T(2,128)} %copy.29), channel_id=1, source_target_pairs={{0,1},{1,0},{2,3},{3,2},{4,5},{5,4},{6,7},{7,6},{8,9},{9,8},{10,11... | collective-permute-start | bytes 17288 | tf_op jit(solution)/shard_map/ppermute | solution.py:15
  285.6 5.7 %collective-permute-start.7 = (f32[2,5,2,36,2]{3,4,2,1,0:T(2,128)S(1)}, f32[2,5,2,36,2]{3,4,2,1,0:T(2,128)}, u32[]{:S(2)}, u32[]{:S(2)}) collective-permute-start(f32[2,5,2,36,2]{3,4,2,1,0:T(2,128)S(1)} %copy.30), channel_id=1, source_target_pairs={{1,0},{0,1},{3,2},{2,3},{5,4},{4,5},{7,6},{6,7},{9,8},{8,9},{11,10... | collective-permute-start | bytes 17288 | tf_op jit(solution)/shard_map/ppermute | solution.py:18
  293.4 1.2 copy-start.2
  300.9 5.6 %collective-permute-start.8 = (f32[2,5,2,2,512]{4,1,3,0,2:T(8,128)S(1)}, f32[2,5,2,2,512]{4,1,3,0,2:T(8,128)S(1)}, u32[]{:S(2)}, u32[]{:S(2)}) collective-permute-start(f32[2,5,2,2,512]{4,1,3,0,2:T(8,128)S(1)} %get-tuple-element.25), channel_id=1, source_target_pairs={{0,2},{2,4},{4,6},{6,8},{8,10},{10,12},{12,14},{14,0},{1,3},{3,5},... | collective-permute-start | bytes 245768 | tf_op jit(solution)/shard_map/ppermute | solution.py:15
  300.9 5.6 %collective-permute-start.9 = (f32[2,5,2,2,512]{4,1,3,0,2:T(8,128)S(1)}, f32[2,5,2,2,512]{4,1,3,0,2:T(8,128)S(1)}, u32[]{:S(2)}, u32[]{:S(2)}) collective-permute-start(f32[2,5,2,2,512]{4,1,3,0,2:T(8,128)S(1)} %get-tuple-element.26), channel_id=1, source_target_pairs={{2,0},{4,2},{6,4},{8,6},{10,8},{12,10},{14,12},{0,14},{3,1},{5,3},... | collective-permute-start | bytes 245768 | tf_op jit(solution)/shard_map/ppermute | solution.py:18
  307.6 5.5 %collective-permute-start.10 = (f32[2,5,2,36,2]{3,4,2,1,0:T(2,128)}, f32[2,5,2,36,2]{3,4,2,1,0:T(2,128)S(1)}, u32[]{:S(2)}, u32[]{:S(2)}) collective-permute-start(f32[2,5,2,36,2]{3,4,2,1,0:T(2,128)} %copy.34), channel_id=1, source_target_pairs={{0,1},{1,0},{2,3},{3,2},{4,5},{5,4},{6,7},{7,6},{8,9},{9,8},{10,11... | collective-permute-start | bytes 17288 | tf_op jit(solution)/shard_map/ppermute | solution.py:15
  308.7 5.5 %collective-permute-start.11 = (f32[2,5,2,36,2]{3,4,2,1,0:T(2,128)S(1)}, f32[2,5,2,36,2]{3,4,2,1,0:T(2,128)}, u32[]{:S(2)}, u32[]{:S(2)}) collective-permute-start(f32[2,5,2,36,2]{3,4,2,1,0:T(2,128)S(1)} %copy.35), channel_id=1, source_target_pairs={{1,0},{0,1},{3,2},{2,3},{5,4},{4,5},{7,6},{6,7},{9,8},{8,9},{11,10... | collective-permute-start | bytes 17288 | tf_op jit(solution)/shard_map/ppermute | solution.py:18
  316.3 1.2 copy-start.3
  323.8 5.6 %collective-permute-start.12 = (f32[2,5,2,2,512]{4,1,3,0,2:T(8,128)S(1)}, f32[2,5,2,2,512]{4,1,3,0,2:T(8,128)S(1)}, u32[]{:S(2)}, u32[]{:S(2)}) collective-permute-start(f32[2,5,2,2,512]{4,1,3,0,2:T(8,128)S(1)} %get-tuple-element.23), channel_id=1, source_target_pairs={{0,2},{2,4},{4,6},{6,8},{8,10},{10,12},{12,14},{14,0},{1,3},{3,5},... | collective-permute-start | bytes 245768 | tf_op jit(solution)/shard_map/ppermute | solution.py:15
  323.8 5.6 %collective-permute-start.13 = (f32[2,5,2,2,512]{4,1,3,0,2:T(8,128)S(1)}, f32[2,5,2,2,512]{4,1,3,0,2:T(8,128)S(1)}, u32[]{:S(2)}, u32[]{:S(2)}) collective-permute-start(f32[2,5,2,2,512]{4,1,3,0,2:T(8,128)S(1)} %get-tuple-element.24), channel_id=1, source_target_pairs={{2,0},{4,2},{6,4},{8,6},{10,8},{12,10},{14,12},{0,14},{3,1},{5,3},... | collective-permute-start | bytes 245768 | tf_op jit(solution)/shard_map/ppermute | solution.py:18
  330.5 5.5 %collective-permute-start.14 = (f32[2,5,2,36,2]{3,4,2,1,0:T(2,128)}, f32[2,5,2,36,2]{3,4,2,1,0:T(2,128)S(1)}, u32[]{:S(2)}, u32[]{:S(2)}) collective-permute-start(f32[2,5,2,36,2]{3,4,2,1,0:T(2,128)} %copy.39), channel_id=1, source_target_pairs={{0,1},{1,0},{2,3},{3,2},{4,5},{5,4},{6,7},{7,6},{8,9},{9,8},{10,11... | collective-permute-start | bytes 17288 | tf_op jit(solution)/shard_map/ppermute | solution.py:15
  333.4 5.7 %collective-permute-start.15 = (f32[2,5,2,36,2]{3,4,2,1,0:T(2,128)S(1)}, f32[2,5,2,36,2]{3,4,2,1,0:T(2,128)}, u32[]{:S(2)}, u32[]{:S(2)}) collective-permute-start(f32[2,5,2,36,2]{3,4,2,1,0:T(2,128)S(1)} %copy.40), channel_id=1, source_target_pairs={{1,0},{0,1},{3,2},{2,3},{5,4},{4,5},{7,6},{6,7},{9,8},{8,9},{11,10... | collective-permute-start | bytes 17288 | tf_op jit(solution)/shard_map/ppermute | solution.py:18
  341.3 1.2 copy-start.4
Sparse Core Ops, SparseCore 0:
  9.1 229.9 all-gather.1
where the time goes:
time: 358 us; the launch traced here: 357 us
  waiting for transfers between devices  254 us (71%)
  starting transfers between devices  26.7 us (7%)
  matrix products  24.9 us (7%)
  local copies, waits for them, and re-layouts  20.8 us (6%)
  other arithmetic  16.9 us (5%)
  between operations  13.8 us (4%)
    all_gather x1, waiting for transfers between devices, shards(): piece = lax.all_gather(state, 'member', axis=0, tiled=True)  231 us
    dot_general x4, matrix products, advance(): jnp.einsum('kvw,mwkij->mvkij', coupling, centre, precision=lax.Precision....  24.9 us
    ppermute x8, starting transfers between devices, with_halo(): lax.ppermute(lax.slice_in_dim(block, 0, width, axis=dim), axis, backward)  17.7 us
    ppermute x8, waiting for transfers between devices, with_halo(): lax.ppermute(lax.slice_in_dim(block, block.shape[dim] - width, None, axis...  16.2 us
    ppermute x8, starting transfers between devices, with_halo(): lax.ppermute(lax.slice_in_dim(block, block.shape[dim] - width, None, axis...  8.97 us
    gather x1, local copies, waits for them, and re-layouts, shards(): rows = jnp.take(piece, jnp.clip(sources, 0, count - 1), axis=0)  7.59 us
  transfers between devices with their start and end apart: 17, of which 12 were waited for; matrix products, arithmetic and copies ran while one was open for 1% of the time, Pallas kernels for 0%

commit v1 on v0

--- a/solution.py
+++ b/solution.py
@@ -48,7 +48,10 @@
     per_dev = state.shape[0]
     group = lax.axis_index("member")
     sources = lax.dynamic_slice_in_dim(clone_src, group * per_dev, per_dev)
-    piece = lax.all_gather(state, "member", axis=0, tiled=True)
+    size = lax.axis_size("member")
+    blocks = jnp.stack([state for _ in range(size)])
+    blocks = lax.all_to_all(blocks, "member", split_axis=0, concat_axis=0)
+    piece = jnp.concatenate(blocks, axis=0)
     count = piece.shape[0]
     inside = (sources >= 0) & (sources < count)
     rows = jnp.take(piece, jnp.clip(sources, 0, count - 1), axis=0)

time: 358 us -> 623 us (1.74)
  the two profiles are of different devices: /device:TPU:4 before, /device:TPU:162 now
where the time goes in v1:
time: 623 us; the launch traced here: 622 us
  waiting for transfers between devices  523 us (84%)
  local copies, waits for them, and re-layouts  31.9 us (5%)
  starting transfers between devices  26 us (4%)
  matrix products  24.9 us (4%)
  other arithmetic  16.2 us (3%)
    all_to_all x1, waiting for transfers between devices, shards(): blocks = lax.all_to_all(blocks, 'member', split_axis=0, concat_axis=0)  490 us
    dot_general x4, matrix products, advance(): jnp.einsum('kvw,mwkij->mvkij', coupling, centre, precision=lax.Precision....  24.9 us
    ppermute x8, waiting for transfers between devices, with_halo(): lax.ppermute(lax.slice_in_dim(block, block.shape[dim] - width, None, axis...  19.5 us
    ppermute x8, waiting for transfers between devices, with_halo(): lax.ppermute(lax.slice_in_dim(block, 0, width, axis=dim), axis, backward)  13 us
  transfers between devices with their start and end apart: 17, of which 17 were waited for; matrix products, arithmetic and copies ran while one was open for 1% of the time, Pallas kernels for 0%

profile of v1, /device:TPU:162, one launch (start us, length us, event | category | flops | bytes accessed | tf_op | source)
XLA Modules:
  0.0 622.1 jit_solution(8952431628556276216)
XLA Ops:
  0.0 11.0 %stack.2 = f32[16,2,5,2,32,512]{5,4,3,2,1,0:T(8,128)} broadcast(f32[2,5,2,32,512]{4,3,2,1,0:T(8,128)} %param.5), dimensions={1,2,3,4,5} | broadcast | bytes 22282240 | tf_op jit(solution)/shard_map/stack | solution.py:52
  11.0 7.8 %all-to-all-start = ((f32[16,2,5,2,32,512]{5,4,3,2,1,0:T(8,128)}), f32[16,2,5,2,32,512]{5,4,3,2,1,0:T(8,128)}, u32[]{:S(2)}, u32[]{:S(2)}) async-start(f32[16,2,5,2,32,512]{5,4,3,2,1,0:T(8,128)} %stack.2), calls=%async_computation | async-start | bytes 41943040 | tf_op jit(solution)/shard_map/all_to_all | solution.py:53
  18.9 490.1 %all-to-all-done = f32[16,2,5,2,32,512]{5,4,3,2,1,0:T(8,128)} async-done(((f32[16,2,5,2,32,512]{5,4,3,2,1,0:T(8,128)}), f32[16,2,5,2,32,512]{5,4,3,2,1,0:T(8,128)}, u32[]{:S(2)}, u32[]{:S(2)}) %all-to-all-start) | async-done | bytes 20971552 | tf_op jit(solution)/shard_map/all_to_all | solution.py:53
  509.0 7.6 %gather_fusion = f32[2,5,2,32,512]{4,3,2,1,0:T(8,128)S(1)} fusion(f32[32,5,2,32,512]{4,3,2,1,0:T(8,128)} %bitcast, s32[1024]{0:T(1024)S(1)} %pad_clamp_fusion), kind=kCustom, calls=%fused_computation | custom fusion | bytes 2621448 | tf_op jit(solution)/shard_map/jit(_take)/gather | solution.py:57
  516.6 3.9 copy_add_fusion
  522.4 2.4 collective-permute-done.1
  524.8 3.2 collective-permute-done
  531.1 2.2 collective-permute-start.3
  536.8 2.1 collective-permute-done.2
  539.3 1.9 maximum_select_fusion
  542.5 6.2 %fusion.7 = f32[2,5,2,32,512]{4,1,3,0,2:T(8,128)S(1)} fusion(f32[2,5,2,36,516]{4,1,3,0,2:T(8,128)S(1)} %maximum_select_fusion, f32[5,2,32,512]{3,0,2,1:T(8,128)S(1)} %copy-done.1, f32[2,2,32,512]{3,2,0,1:T(8,128)S(1)} %get-tuple-element.32, f32[2,2,32,512]{3,2,0,1:T(8,128)S(1)} %get-tuple-element.33, f32[2,5,5,1,1]{2,0,1,4,3:T(2,128)S(1)} %bitcast.51), kind=kOutput, calls=%fused_computation.16 | convolution fusion | flops 28835840 | bytes 23860224 | tf_op jit(solution)/shard_map/kvw,mwkij->mvkij/dot_general | solution.py:38
  549.3 2.0 collective-permute-done.5
  551.3 3.1 collective-permute-done.4
  557.1 2.4 collective-permute-start.6
  566.1 6.2 %fusion.5 = f32[2,5,2,32,512]{4,1,3,0,2:T(8,128)S(1)} fusion(f32[2,5,2,36,516]{4,1,3,0,2:T(8,128)S(1)} %maximum_select_fusion.1, f32[2,2,32,512]{3,2,0,1:T(8,128)S(1)} %bitcast.56, f32[2,2,32,512]{3,2,0,1:T(8,128)S(1)} %bitcast.59, f32[5,2,32,512]{3,0,2,1:T(8,128)S(1)} %copy-done.2, f32[2,5,5,1,1]{2,0,1,4,3:T(2,128)S(1)} %bitcast.54), kind=kOutput, calls=%fused_computation.13 | convolution fusion | flops 28835840 | bytes 23860224 | tf_op jit(solution)/shard_map/kvw,mwkij->mvkij/dot_general | solution.py:38
  572.9 2.0 collective-permute-done.9
  574.9 3.1 collective-permute-done.8
  579.1 2.1 collective-permute-start.11
  585.0 2.0 collective-permute-done.10
  590.3 6.2 %fusion.3 = f32[2,5,2,32,512]{4,1,3,0,2:T(8,128)S(1)} fusion(f32[2,5,2,36,516]{4,1,3,0,2:T(8,128)S(1)} %maximum_select_fusion.2, f32[2,2,32,512]{3,2,0,1:T(8,128)S(1)} %bitcast.57, f32[2,2,32,512]{3,2,0,1:T(8,128)S(1)} %bitcast.60, f32[5,2,32,512]{3,0,2,1:T(8,128)S(1)} %copy-done.3, f32[2,5,5,1,1]{2,0,1,4,3:T(2,128)S(1)} %bitcast.53), kind=kOutput, calls=%fused_computation.10 | convolution fusion | flops 28835840 | bytes 23860224 | tf_op jit(solution)/shard_map/kvw,mwkij->mvkij/dot_general | solution.py:38
  597.1 2.0 collective-permute-done.13
  599.1 3.1 collective-permute-done.12
  605.0 2.4 collective-permute-start.14
  614.0 6.2 fusion.1
  (76 shorter events, 40.3 us)
Async XLA Ops:
  0.0 542.4 %copy-start = (f32[2,5,5]{2,0,1:T(2,128)S(1)}, f32[2,5,5]{2,0,1:T(2,128)}, u32[]{:S(2)}) copy-start(f32[2,5,5]{2,0,1:T(2,128)} %param.8) | copy-start | bytes 604
  11.0 7.8 %copy-start.6 = (s32[32]{0:T(128)S(1)}, s32[32]{0:T(128)}, u32[]{:S(2)}) copy-start(s32[32]{0:T(128)} %param.9) | copy-start | bytes 388
  11.0 498.0 %all-to-all-start = ((f32[16,2,5,2,32,512]{5,4,3,2,1,0:T(8,128)}), f32[16,2,5,2,32,512]{5,4,3,2,1,0:T(8,128)}, u32[]{:S(2)}, u32[]{:S(2)}) async-start(f32[16,2,5,2,32,512]{5,4,3,2,1,0:T(8,128)} %stack.2), calls=%async_computation | async-start | bytes 41943040 | tf_op jit(solution)/shard_map/all_to_all | solution.py:53
  516.6 5.7 copy-start.5
  520.5 4.3 collective-permute-start.1
  522.3 5.7 collective-permute-start
  531.1 5.4 collective-permute-start.3
  533.6 5.4 collective-permute-start.2
  541.2 1.2 copy-start.1
  548.7 2.5 collective-permute-start.5
  548.8 5.6 collective-permute-start.4
  555.4 5.5 collective-permute-start.7
  557.1 5.7 collective-permute-start.6
  564.9 1.2 copy-start.2
  572.4 2.5 collective-permute-start.9
  572.4 5.6 collective-permute-start.8
  579.1 5.5 collective-permute-start.11
  581.5 5.5 collective-permute-start.10
  589.1 1.2 copy-start.3
  596.6 2.5 collective-permute-start.13
  596.6 5.6 collective-permute-start.12
  603.3 5.5 collective-permute-start.15
  605.0 5.7 collective-permute-start.14
  612.8 1.2 copy-start.4
